TPU v7x, 256 devices: a whole 4x4x8 slice. The times are simulated.
256 devices in a mesh: seq: 32 (over z, y), ffn: 8 (over x, core).
Axes of the slice: x: 4, y: 4, z: 8, core: 2. Of those that a mesh axis runs over, the one named last changes fastest.
Arguments:
- patches: bfloat16 [8192, 4096], P('seq'), may hold values from -100 to 100
- gate_weight: bfloat16 [4096, 7168], P('seq', 'ffn'), may hold values from -0.09375 to 0.09375
- up_weight: bfloat16 [4096, 7168], P('seq', 'ffn'), may hold values from -0.09375 to 0.09375
- down_weight: bfloat16 [4096, 7168], P('seq', 'ffn'), may hold values from -0.25 to 0.25
- key_weight: bfloat16 [4096, 1024], P(None, 'ffn'), may hold values from -0.09375 to 0.09375
- value_weight: bfloat16 [4096, 1024], P(None, 'ffn'), may hold values from -0.09375 to 0.09375
- byte_states: bfloat16 [65536, 1024], P('seq'), may hold values from -60 to 60
- byte_patch: int32 [65536], P('seq'), may hold values from 0 to 8191, as said below
- cross_query: bfloat16 [1024, 1024], P(None, 'ffn'), may hold values from -0.375 to 0.375
- self_query: bfloat16 [1024, 1024], P(None, 'ffn'), may hold values from -0.375 to 0.375
- self_key: bfloat16 [1024, 1024], P(None, 'ffn'), may hold values from -0.375 to 0.375
- self_value: bfloat16 [1024, 1024], P(None, 'ffn'), may hold values from -0.1875 to 0.1875
- cross_out: bfloat16 [1024, 1024], P('ffn'), may hold values from -0.1875 to 0.1875
- self_out: bfloat16 [1024, 1024], P('ffn'), may hold values from -0.1875 to 0.1875
Outputs:
- update: bfloat16 [65536, 1024], P('seq', 'ffn')
Inputs may be any that keep to these rules, and one draw needn't show every extreme that they name: byte_patch starts at 0, never falls, rises by at most 1 from one byte to the next and ends at 8191, so every patch is a run of one or more bytes. The bytes s * 2048 to (s + 1) * 2048 - 1 read only patches s * 256 - 23 to (s + 1) * 256 + 15; both ends are reached in every draw.
All inputs are finite; a program needn't handle non-finite values.
Results may differ from a plain program's by a relative error of at most 0.0085.
The roundings to bfloat16 on the way count: a program that leaves them out, or rounds other values in their place, can miss the bound.
Values may be sent and summed in bfloat16 or wider, within the bound.
No kernel may reach another device: no remote copies, remote signals or barrier semaphores. Data moves between devices by JAX's collectives and lax.ppermute only.
A program may use at most 128 MiB of HBM per device.

v0:
```python
import math
import jax
import jax.numpy as jnp
from jax import lax
from jax.sharding import PartitionSpec as P

HD = 64
PWIN = 8
WINDOW = 512
HALO = 23
EPS = 1e-05


def padded(value, sides, width):
    for axis, dim in sides:
        count, length = (lax.axis_size(axis), value.shape[dim])
        up = [(i, (i + 1) % count) for i in range(count - 1)]
        down = [(j, i) for i, j in up]
        last = lax.slice_in_dim(value, length - width, length, axis=dim)
        first = lax.slice_in_dim(value, 0, width, axis=dim)
        before = lax.ppermute(last, axis, up)
        after = lax.ppermute(first, axis, down)
        value = jnp.concatenate([before, value, after], axis=dim)
    return value


def shifted(value, axis, by):
    count = lax.axis_size(axis)
    pairs = [(i, i + by) for i in range(count) if 0 <= i + by < count]
    return lax.ppermute(value, axis, pairs)


def row_normalize(matrix):
    widened = matrix.astype(jnp.float32)
    return widened * lax.rsqrt(jnp.mean(widened * widened, axis=-1, keepdims=True) + EPS)


def masked_softmax(scores, key_mask):
    masked = jnp.where(key_mask, scores, -jnp.inf)
    row_max = jnp.max(masked, axis=-1, keepdims=True)
    exp_terms = jnp.exp(masked - row_max)
    return exp_terms / jnp.sum(exp_terms, axis=-1, keepdims=True)


def local(
    patches,
    gate_weight,
    up_weight,
    down_weight,
    key_weight,
    value_weight,
    byte_states,
    byte_patch,
    cross_query,
    self_query,
    self_key,
    self_value,
    cross_out,
    self_out,
):
    patch_count = patches.shape[0]
    normed = row_normalize(patches).astype(jnp.bfloat16)

    def add_rows(piece_rows):
        return jnp.dot(normed, piece_rows, preferred_element_type=jnp.float32)

    gate_sum = add_rows(lax.all_gather(gate_weight, "seq", axis=0, tiled=True))
    up_sum = add_rows(lax.all_gather(up_weight, "seq", axis=0, tiled=True))
    hidden = (jax.nn.silu(gate_sum) * up_sum).astype(jnp.bfloat16)
    ffn_out = lax.dot_general(
        hidden,
        lax.all_gather(down_weight, "seq", axis=0, tiled=True),
        (((1,), (1,)), ((), ())),
        preferred_element_type=jnp.float32,
    )
    ffn_whole = lax.psum(ffn_out, "ffn")
    global_out = (patches.astype(jnp.float32) + ffn_whole).astype(jnp.bfloat16)
    head_cols = key_weight.shape[1]
    head_count = head_cols // HD
    score_scale = 1.0 / math.sqrt(HD)
    seq_index = lax.axis_index("seq")
    keys_c = jnp.dot(global_out, key_weight, preferred_element_type=jnp.float32).astype(
        jnp.bfloat16
    )
    values_c = jnp.dot(global_out, value_weight, preferred_element_type=jnp.float32).astype(
        jnp.bfloat16
    )
    both_c = jnp.concatenate([keys_c, values_c], axis=1)
    extended = padded(both_c, (("seq", 0),), HALO)
    key_count = extended.shape[0]
    key_index = seq_index * patch_count - HALO + jnp.arange(key_count, dtype=jnp.int32)
    cross_mask = (
        (key_index[None, :] <= byte_patch[:, None])
        & (key_index[None, :] > byte_patch[:, None] - PWIN)
        & (key_index[None, :] >= 0)
    )
    byte_count = byte_states.shape[0]
    query_c = jnp.dot(byte_states, cross_query, preferred_element_type=jnp.float32).astype(
        jnp.bfloat16
    )
    query_s = jnp.dot(byte_states, self_query, preferred_element_type=jnp.float32).astype(
        jnp.bfloat16
    )
    keys_s = jnp.dot(byte_states, self_key, preferred_element_type=jnp.float32).astype(jnp.bfloat16)
    values_s = jnp.dot(byte_states, self_value, preferred_element_type=jnp.float32).astype(
        jnp.bfloat16
    )
    query_here = query_c.reshape(byte_count, head_count, HD)
    keys_here = extended[:, :head_cols].reshape(key_count, head_count, HD)
    values_here = extended[:, head_cols:].reshape(key_count, head_count, HD)
    cross_scores = (
        jnp.einsum("qhd,khd->hqk", query_here, keys_here, preferred_element_type=jnp.float32)
        * score_scale
    )
    weights_c = masked_softmax(cross_scores, cross_mask[None]).astype(jnp.bfloat16)
    context_c = jnp.einsum(
        "hqk,khd->qhd", weights_c, values_here, preferred_element_type=jnp.float32
    )
    context_c = context_c.astype(jnp.bfloat16).reshape(byte_count, head_cols)
    both_s = jnp.concatenate([keys_s, values_s], axis=1)
    tail_rows = both_s[byte_count - WINDOW :]
    before = shifted(tail_rows, "seq", 1)
    stacked = jnp.concatenate([before, both_s], axis=0)
    blocks = byte_count // WINDOW
    lower_half = stacked[:byte_count].reshape(blocks, WINDOW, 2 * head_cols)
    upper_half = stacked[WINDOW:].reshape(blocks, WINDOW, 2 * head_cols)
    key_pairs = jnp.concatenate([lower_half, upper_half], axis=1)
    window_keys = key_pairs[:, :, :head_cols].reshape(blocks, 2 * WINDOW, head_count, HD)
    window_values = key_pairs[:, :, head_cols:].reshape(blocks, 2 * WINDOW, head_count, HD)
    window_queries = query_s.reshape(blocks, WINDOW, head_count, HD)
    self_scores = (
        jnp.einsum(
            "bqhd,bkhd->bhqk", window_queries, window_keys, preferred_element_type=jnp.float32
        )
        * score_scale
    )
    query_slot = jnp.arange(WINDOW, dtype=jnp.int32)[:, None]
    key_slot = jnp.arange(2 * WINDOW, dtype=jnp.int32)[None, :]
    band_mask = (key_slot > query_slot) & (key_slot <= query_slot + WINDOW)
    block_ids = jnp.arange(blocks, dtype=jnp.int32)
    key_pos = (
        seq_index * byte_count
        - WINDOW
        + block_ids[:, None] * WINDOW
        + jnp.arange(2 * WINDOW, dtype=jnp.int32)[None, :]
    )
    self_mask = band_mask[None, None] & (key_pos >= 0)[:, None, None, :]
    weights_s = masked_softmax(self_scores, self_mask).astype(jnp.bfloat16)
    context_s = jnp.einsum(
        "bhqk,bkhd->bqhd", weights_s, window_values, preferred_element_type=jnp.float32
    )
    context_s = context_s.astype(jnp.bfloat16).reshape(byte_count, head_cols)
    partial_sum = jnp.dot(context_c, cross_out, preferred_element_type=jnp.float32) + jnp.dot(
        context_s, self_out, preferred_element_type=jnp.float32
    )
    return lax.psum_scatter(partial_sum, "ffn", scatter_dimension=1, tiled=True).astype(
        jnp.bfloat16
    )


def solution(mesh):
    placed = (
        P("seq", None),
        P("seq", "ffn"),
        P("seq", "ffn"),
        P("seq", "ffn"),
        P(None, "ffn"),
        P(None, "ffn"),
        P("seq", None),
        P("seq"),
        P(None, "ffn"),
        P(None, "ffn"),
        P(None, "ffn"),
        P(None, "ffn"),
        P("ffn", None),
        P("ffn", None),
    )
    return jax.shard_map(
        local, mesh=mesh, in_specs=placed, out_specs=P("seq", "ffn"), check_vma=False
    )
```

profile of v0, /device:TPU:1, one launch (start us, length us, event | category | flops | bytes accessed | tf_op | source)
XLA Modules:
  0.0 472.8 jit_solution(5095927345951818433)
XLA Ops:
  6.5 0.7 all-gather.4.cloned.1.call-update
  7.3 0.0 all-gather.6.cloned.1.call-start
  7.3 0.7 all-gather.6.cloned.1.call-update
  8.0 0.0 all-gather.8.cloned.1.call-start
  8.1 0.7 all-gather.8.cloned.1.call-update
  8.7 0.0 all-reduce.2.cloned.1.call-start
  8.8 0.0 copy-start.2
  8.8 3.9 convolution_convert_fusion.2
  12.7 0.0 copy-start.16
  12.7 0.0 copy-start.14
  12.7 1.5 convolution_convert_fusion.1
  14.3 0.8 copy-done.7
  15.1 4.7 collective-permute-start.2
  19.9 0.1 add_compare_fusion
  19.9 0.0 copy-done.16
  20.0 0.4 fusion.16
  20.4 4.8 %convolution_convert_fusion.3 = bf16[2048,128]{0,1:T(8,128)(2,1)} fusion(bf16[2048,1024]{1,0:T(8,128)(2,1)} %param.20, bf16[1024,128]{1,0:T(8,128)(2,1)S(1)} %copy-done.14), kind=kOutput, calls=%fused_computation.31 | convolution fusion | flops 537133056 | bytes 4980736 | tf_op jit(solution)/shard_map/dot_general | solution.py:98
  25.1 0.0 copy-done.3
  25.1 3.2 convolution_convert_fusion
  28.3 1.5 and_and_fusion
  29.8 2.3 broadcast_and_fusion
  32.1 0.0 copy-done.4
  32.1 0.5 fusion.7
  32.6 3.4 reshape.197
  36.0 0.0 collective-permute-done.2
  36.0 3.3 pad_maximum_fusion
  39.2 2.6 reshape.191
  41.9 64.2 %all-gather.4.cloned.1.call-done = bf16[4096,896]{1,0:T(8,128)(2,1)} async-done(((bf16[128,896]{1,0:T(8,128)(2,1)}), bf16[4096,896]{1,0:T(8,128)(2,1)}) %all-gather.4.cloned.1.call-update) | async-done | bytes 7340048 | tf_op jit(solution)/shard_map/all_gather | solution.py:67
  106.1 6.4 %fusion.30 = f32[256,896]{1,0:T(8,128)} fusion(bf16[4096,896]{1,0:T(8,128)(2,1)} %all-gather.4.cloned.1.call-done, bf16[256,4096]{1,0:T(8,128)(2,1)S(1)} %copy-done.4, f32[256]{0:T(256)S(1)} %add_rsqrt_fusion), kind=kOutput, calls=%fused_computation.50 | convolution fusion | flops 1882193920 | bytes 10355712 | tf_op jit(solution)/shard_map/dot_general | solution.py:65
  112.5 86.2 %all-gather.6.cloned.1.call-done = bf16[4096,896]{1,0:T(8,128)(2,1)} async-done(((bf16[128,896]{1,0:T(8,128)(2,1)}), bf16[4096,896]{1,0:T(8,128)(2,1)}) %all-gather.6.cloned.1.call-update) | async-done | bytes 7340048 | tf_op jit(solution)/shard_map/all_gather | solution.py:68
  198.8 92.7 %all-gather.8.cloned.1.call-done = bf16[4096,896]{1,0:T(8,128)(2,1)} async-done(((bf16[128,896]{1,0:T(8,128)(2,1)}), bf16[4096,896]{1,0:T(8,128)(2,1)}) %all-gather.8.cloned.1.call-update) | async-done | bytes 7340048 | tf_op jit(solution)/shard_map/all_gather | solution.py:72
  291.4 12.0 %fusion.35 = f32[256,4096]{1,0:T(8,128)} fusion(bf16[4096,896]{1,0:T(8,128)(2,1)} %all-gather.8.cloned.1.call-done, bf16[4096,896]{1,0:T(8,128)(2,1)} %all-gather.6.cloned.1.call-done, f32[256,896]{1,0:T(8,128)} %fusion.30, bf16[256,4096]{1,0:T(8,128)(2,1)S(1)} %copy-done.4, f32[256]{0:T(256)S(1)} %add_rsqrt_fusion), kind=kOutput, calls=%fused_computation.52 | convolution fusion | flops 3762618368 | bytes 21890048 | tf_op jit(solution)/shard_map/dot_general | solution.py:70
  303.4 0.0 all-reduce.2.cloned.1.call-update
  303.5 0.0 reduce-scatter.2.cloned.1.call-start
  303.5 2.6 constant_dynamic-update-slice_fusion.1
  306.1 2.6 reshape.192
  308.8 2.6 constant_dynamic-update-slice_fusion
  311.3 2.6 fusion.51
  313.9 1.4 copy.20
  315.3 1.3 copy.18
  316.6 11.0 %fusion.54 = (f32[4,2,512]{2,1,0:T(2,128)S(1)}, f32[4,2,512,1024]{3,2,1,0:T(8,128)}) fusion(pred[4,512,1024]{2,1,0:T(8,128)(4,1)} %broadcast_and_fusion, bf16[4,1024,2,64]{1,3,2,0:T(8,128)(2,1)} %bitcast.47, bf16[4,512,2,64]{3,2,1,0:T(2,128)(2,1)} %reshape.197), kind=kOutput, calls=%fused_computation.79 | convolution fusion | flops 553649152 | bytes 20463616 | tf_op jit(solution)/shard_map/sub | solution.py:41
  327.6 49.4 %all-reduce.2.cloned.1.call-done = f32[256,4096]{1,0:T(8,128)} async-done(((f32[256,4096]{1,0:T(8,128)}), f32[256,4096]{1,0:T(8,128)}) %all-reduce.2.cloned.1.call-update) | async-done | bytes 4194320 | tf_op jit(solution)/shard_map/psum | solution.py:76
  377.0 3.1 convolution_convert_fusion.4
  380.2 0.3 copy-done.5
  380.5 0.3 copy-done.8
  380.8 0.9 convolution_convert_fusion.5
  381.6 0.1 fusion.39
  381.7 3.1 collective-permute-start
  384.8 1.6 collective-permute-start.1
  386.4 0.0 copy-start.11
  386.4 8.6 %fusion.21 = bf16[4,512,2,64]{1,3,2,0:T(8,128)(2,1)S(1)} fusion(bf16[4,1024,2,64]{1,3,2,0:T(8,128)(2,1)S(1)} %bitcast.46, f32[4,2,512,1024]{3,2,1,0:T(8,128)} %get-tuple-element.14, f32[4,2,512]{2,1,0:T(2,128)S(1)} %get-tuple-element.13), kind=kOutput, calls=%fused_computation.39 | convolution fusion | flops 545521664 | bytes 18366464 | tf_op jit(solution)/shard_map/bhqk,bkhd->bqhd/dot_general | solution.py:149
  395.0 0.4 copy.22
  395.4 0.1 copy.25
  395.5 0.0 collective-permute-done
  395.6 0.0 collective-permute-done.1
  395.6 0.1 pad_maximum_fusion.3
  395.8 1.8 fusion.53
  397.6 2.5 fusion.15
  400.2 0.0 copy-start.12
  400.2 1.3 fusion.59
  401.5 4.5 convolution_add_fusion
  406.0 0.0 reduce-scatter.2.cloned.1.call-update
  406.0 58.2 %reduce-scatter.2.cloned.1.call-done = f32[2048,128]{1,0:T(8,128)} async-done(((f32[2048,1024]{1,0:T(8,128)}), f32[2048,128]{1,0:T(8,128)}) %reduce-scatter.2.cloned.1.call-update) | async-done | bytes 1048592 | tf_op jit(solution)/shard_map/reduce_scatter | solution.py:156
  464.2 2.1 convert_element_type.68
  (32 shorter events, 0.1 us)
Async XLA Ops:
  6.5 370.5 %copy-start = (bf16[4096,128]{1,0:T(8,128)(2,1)S(1)}, bf16[4096,128]{1,0:T(8,128)(2,1)}, u32[]{:S(2)}) copy-start(bf16[4096,128]{1,0:T(8,128)(2,1)} %param.19) | copy-start | bytes 3145732
  6.5 6.1 %copy-start.13 = (bf16[1024,128]{1,0:T(8,128)(2,1)S(1)}, bf16[1024,128]{1,0:T(8,128)(2,1)}, u32[]{:S(2)}) copy-start(bf16[1024,128]{1,0:T(8,128)(2,1)} %param.25) | copy-start | bytes 786436
  6.5 99.6 %all-gather.4.cloned.1.call-start = ((), (), s32[]{:S(2)}) async-start(), calls=%async_computation.1 | async-start | bytes 7569408 | tf_op jit(solution)/shard_map/all_gather | solution.py:67
  7.3 191.5 %all-gather.6.cloned.1.call-start = ((), (), s32[]{:S(2)}) async-start(), calls=%async_computation.2 | async-start | bytes 7569408 | tf_op jit(solution)/shard_map/all_gather | solution.py:68
  8.0 283.4 %all-gather.8.cloned.1.call-start = ((), (), s32[]{:S(2)}) async-start(), calls=%async_computation.3 | async-start | bytes 7569408 | tf_op jit(solution)/shard_map/all_gather | solution.py:72
  8.7 368.3 %all-reduce.2.cloned.1.call-start = ((), (), s32[]{:S(2)}) async-start(), calls=%async_computation.4 | async-start | bytes 8388608 | tf_op jit(solution)/shard_map/psum | solution.py:76
  8.8 3.9 copy-start.2
  12.7 1.6 copy-start.6
  12.7 7.2 %copy-start.16 = (s32[2048]{0:T(1024)S(1)}, s32[2048]{0:T(1024)}, u32[]{:S(2)}) copy-start(s32[2048]{0:T(1024)} %param.21) | copy-start | bytes 24580
  12.7 7.6 %copy-start.14 = (bf16[1024,128]{1,0:T(8,128)(2,1)S(1)}, bf16[1024,128]{1,0:T(8,128)(2,1)}, u32[]{:S(2)}) copy-start(bf16[1024,128]{1,0:T(8,128)(2,1)} %param.22) | copy-start | bytes 786436
  14.3 0.8 copy-start.7
  15.1 20.8 %collective-permute-start.2 = (bf16[512,256]{0,1:T(8,128)(2,1)S(1)}, bf16[512,256]{0,1:T(8,128)(2,1)}, u32[]{:S(2)}, u32[]{:S(2)}) collective-permute-start(bf16[512,256]{0,1:T(8,128)(2,1)S(1)} %fusion.38), channel_id=1, source_target_pairs={{0,8},{8,16},{16,24},{24,32},{32,40},{40,48},{48,56},{56,64},{64,7... | collective-permute-start | bytes 786440 | tf_op jit(solution)/shard_map/ppermute | solution.py:30
  19.8 5.3 %copy-start.3 = (bf16[2048,1024]{1,0:T(8,128)(2,1)S(1)}, bf16[2048,1024]{1,0:T(8,128)(2,1)}, u32[]{:S(2)}) copy-start(bf16[2048,1024]{1,0:T(8,128)(2,1)} %param.20) | copy-start | bytes 12582916
  25.1 7.0 %copy-start.4 = (bf16[256,4096]{1,0:T(8,128)(2,1)S(1)}, bf16[256,4096]{1,0:T(8,128)(2,1)}, u32[]{:S(2)}) copy-start(bf16[256,4096]{1,0:T(8,128)(2,1)} %param.14) | copy-start | bytes 6291460
  303.5 160.7 %reduce-scatter.2.cloned.1.call-start = ((), (), s32[]{:S(2)}) async-start(), calls=%async_computation.5 | async-start | bytes 9437184 | tf_op jit(solution)/shard_map/reduce_scatter | solution.py:156
  377.0 3.4 copy-start.5
  377.0 3.7 copy-start.8
  380.8 5.7 %copy-start.9 = (bf16[4,1024,128]{1,2,0:T(8,128)(2,1)S(1)}, bf16[4,1024,128]{1,2,0:T(8,128)(2,1)}, u32[]{:S(2)}) copy-start(bf16[4,1024,128]{1,2,0:T(8,128)(2,1)} %copy.18) | copy-start | bytes 3145732
  381.7 13.8 %collective-permute-start = (bf16[23,256]{0,1:T(8,128)(2,1)S(1)}, bf16[23,256]{0,1:T(8,128)(2,1)S(1)}, u32[]{:S(2)}, u32[]{:S(2)}) collective-permute-start(bf16[23,256]{0,1:T(8,128)(2,1)S(1)} %get-tuple-element.11), channel_id=1, source_target_pairs={{0,8},{8,16},{16,24},{24,32},{32,40},{40,48},{48,56},{56,64},{64,7... | collective-permute-start | bytes 35336 | tf_op jit(solution)/shard_map/ppermute | solution.py:21
  384.8 10.7 %collective-permute-start.1 = (bf16[23,256]{0,1:T(8,128)(2,1)S(1)}, bf16[23,256]{0,1:T(8,128)(2,1)S(1)}, u32[]{:S(2)}, u32[]{:S(2)}) collective-permute-start(bf16[23,256]{0,1:T(8,128)(2,1)S(1)} %get-tuple-element.12), channel_id=1, source_target_pairs={{8,0},{16,8},{24,16},{32,24},{40,32},{48,40},{56,48},{64,56},{72,6... | collective-permute-start | bytes 35336 | tf_op jit(solution)/shard_map/ppermute | solution.py:22
  386.4 9.3 %copy-start.10 = (pred[2048,302]{0,1:T(8,128)(4,1)S(1)}, pred[2048,302]{0,1:T(8,128)(4,1)}, u32[]{:S(2)}) copy-start(pred[2048,302]{0,1:T(8,128)(4,1)} %and_and_fusion) | copy-start | bytes 1855492
  386.4 9.3 %copy-start.11 = (bf16[2048,128]{0,1:T(8,128)(2,1)S(1)}, bf16[2048,128]{0,1:T(8,128)(2,1)}, u32[]{:S(2)}) copy-start(bf16[2048,128]{0,1:T(8,128)(2,1)} %convolution_convert_fusion.3) | copy-start | bytes 1572868
  397.6 2.5 copy-start.15
  400.2 1.3 copy-start.12
  406.0 60.3 %copy-start.1 = (bf16[4096,128]{1,0:T(8,128)(2,1)S(1)}, bf16[4096,128]{1,0:T(8,128)(2,1)}, u32[]{:S(2)}) copy-start(bf16[4096,128]{1,0:T(8,128)(2,1)} %param.19) | copy-start | bytes 3145732
Sparse Core Ops, SparseCore 0:
  9.9 96.1 all-gather.3
  108.7 90.0 all-gather.5
  201.3 90.0 all-gather.7
  303.6 73.3 all-reduce.1
  406.1 58.0 reduce-scatter.1
where the time goes:
time: 473 us
  waiting for transfers between devices  353 us (75%)
  matrix products  65.5 us (14%)
  local copies, waits for them, and re-layouts  21.1 us (4%)
  between operations  13.5 us (3%)
  other arithmetic  10.4 us (2%)
  starting transfers between devices  9.53 us (2%)
    all_gather x1, waiting for transfers between devices, local(): lax.all_gather(down_weight, 'seq', axis=0, tiled=True)  92.7 us
    all_gather x1, waiting for transfers between devices, local(): up_sum = add_rows(lax.all_gather(up_weight, 'seq', axis=0, tiled=True))  86.2 us
    all_gather x1, waiting for transfers between devices, local(): gate_sum = add_rows(lax.all_gather(gate_weight, 'seq', axis=0, tiled=True))  64.2 us
    reduce_scatter x1, waiting for transfers between devices, local(): lax.psum_scatter(partial_sum, 'ffn', scatter_dimension=1, tiled=True)  58.2 us
    psum x1, waiting for transfers between devices, local(): ffn_whole = lax.psum(ffn_out, 'ffn')  49.4 us
    sub x2, matrix products, masked_softmax(): exp_terms = jnp.exp(masked - row_max)  12.8 us
    dot_general x1, matrix products, local(): lax.dot_general(hidden, lax.all_gather(down_weight, 'seq', axis=0, tiled=...  12 us
  transfers between devices with their start and end apart: 8, of which 5 were waited for; matrix products, arithmetic and copies ran while one was open for 14% of the time, Pallas kernels for 0%

commit v1 on v0

--- a/solution.py
+++ b/solution.py
@@ -73,7 +73,7 @@
         (((1,), (1,)), ((), ())),
         preferred_element_type=jnp.float32,
     )
-    ffn_whole = lax.psum(ffn_out, "ffn")
+    ffn_whole = jnp.sum(lax.all_gather(ffn_out, "ffn"), axis=0)
     global_out = (patches.astype(jnp.float32) + ffn_whole).astype(jnp.bfloat16)
     head_cols = key_weight.shape[1]
     head_count = head_cols // HD

time: 473 us -> 572 us (1.21)
  waiting for transfers between devices: 353 us -> 437 us
  other arithmetic: 10.4 us -> 26.2 us
    all_gather x0 -> x1, waiting for transfers between devices: none -> 104 us  [local(): ffn_whole = jnp.sum(lax.all_gather(ffn_out, 'ffn'), axis=0)]
    psum x1 -> x0, waiting for transfers between devices: 49.4 us -> none  [local(): ffn_whole = lax.psum(ffn_out, 'ffn')]
    all_gather x1, waiting for transfers between devices: 64.2 us -> 95.2 us  [local(): gate_sum = add_rows(lax.all_gather(gate_weight, 'seq', axis=0, tiled=True))]
    reduce_sum x0 -> x1, other arithmetic: none -> 14.3 us  [local(): ffn_whole = jnp.sum(lax.all_gather(ffn_out, 'ffn'), axis=0)]
    all_gather x1, waiting for transfers between devices: 92.7 us -> 85.6 us  [local(): lax.all_gather(down_weight, 'seq', axis=0, tiled=True)]
    all_gather x1, waiting for transfers between devices: 86.2 us -> 92.7 us  [local(): up_sum = add_rows(lax.all_gather(up_weight, 'seq', axis=0, tiled=True))]
  transfers between devices with their start and end apart: 8 -> 8, of which waited for: 5 -> 5; matrix products, arithmetic and copies ran while one was open for 14% -> 12% of each run, Pallas kernels for 0% -> 0%
where the time goes in v1:
time: 572 us; the launch traced here: 571 us
  waiting for transfers between devices  437 us (76%)
  matrix products  68.7 us (12%)
  other arithmetic  26.2 us (5%)
  local copies, waits for them, and re-layouts  18.1 us (3%)
  between operations  13.5 us (2%)
  starting transfers between devices  7.24 us (1%)
    all_gather x1, waiting for transfers between devices, local(): ffn_whole = jnp.sum(lax.all_gather(ffn_out, 'ffn'), axis=0)  104 us
    all_gather x1, waiting for transfers between devices, local(): gate_sum = add_rows(lax.all_gather(gate_weight, 'seq', axis=0, tiled=True))  95.2 us
    all_gather x1, waiting for transfers between devices, local(): up_sum = add_rows(lax.all_gather(up_weight, 'seq', axis=0, tiled=True))  92.7 us
    all_gather x1, waiting for transfers between devices, local(): lax.all_gather(down_weight, 'seq', axis=0, tiled=True)  85.6 us
    reduce_scatter x1, waiting for transfers between devices, local(): lax.psum_scatter(partial_sum, 'ffn', scatter_dimension=1, tiled=True)  57.5 us
    reduce_sum x1, other arithmetic, local(): ffn_whole = jnp.sum(lax.all_gather(ffn_out, 'ffn'), axis=0)  14.3 us
    sub x2, matrix products, masked_softmax(): exp_terms = jnp.exp(masked - row_max)  12.8 us
    dot_general x1, matrix products, local(): lax.dot_general(hidden, lax.all_gather(down_weight, 'seq', axis=0, tiled=...  12.1 us
  transfers between devices with their start and end apart: 8, of which 5 were waited for; matrix products, arithmetic and copies ran while one was open for 12% of the time, Pallas kernels for 0%

profile of v1, /device:TPU:1, one launch (start us, length us, event | category | flops | bytes accessed | tf_op | source)
XLA Modules:
  0.0 571.0 jit_solution(16748611505055909145)
XLA Ops:
  6.5 0.7 all-gather.6.cloned.1.call-update
  7.3 0.0 all-gather.10.cloned.1.call-start
  7.3 0.7 all-gather.10.cloned.1.call-update
  8.0 0.0 all-gather.8.cloned.1.call-start
  8.1 0.7 all-gather.8.cloned.1.call-update
  8.7 0.0 all-gather.12.cloned.1.call-start
  8.8 2.1 fusion.7
  10.9 0.0 copy-start.3
  10.9 95.2 %all-gather.6.cloned.1.call-done = bf16[4096,896]{1,0:T(8,128)(2,1)} async-done(((bf16[128,896]{1,0:T(8,128)(2,1)}), bf16[4096,896]{1,0:T(8,128)(2,1)}) %all-gather.6.cloned.1.call-update) | async-done | bytes 7340048 | tf_op jit(solution)/shard_map/all_gather | solution.py:67
  106.1 7.0 %fusion.30 = f32[256,896]{1,0:T(8,128)} fusion(bf16[4096,896]{1,0:T(8,128)(2,1)} %all-gather.6.cloned.1.call-done, bf16[256,4096]{1,0:T(8,128)(2,1)} %param.14, f32[256]{0:T(256)S(1)} %add_rsqrt_fusion), kind=kOutput, calls=%fused_computation.50 | convolution fusion | flops 1882193920 | bytes 10355712 | tf_op jit(solution)/shard_map/dot_general | solution.py:65
  113.1 85.6 %all-gather.10.cloned.1.call-done = bf16[4096,896]{1,0:T(8,128)(2,1)} async-done(((bf16[128,896]{1,0:T(8,128)(2,1)}), bf16[4096,896]{1,0:T(8,128)(2,1)}) %all-gather.10.cloned.1.call-update) | async-done | bytes 7340048 | tf_op jit(solution)/shard_map/all_gather | solution.py:72
  198.8 92.7 %all-gather.8.cloned.1.call-done = bf16[4096,896]{1,0:T(8,128)(2,1)} async-done(((bf16[128,896]{1,0:T(8,128)(2,1)}), bf16[4096,896]{1,0:T(8,128)(2,1)}) %all-gather.8.cloned.1.call-update) | async-done | bytes 7340048 | tf_op jit(solution)/shard_map/all_gather | solution.py:68
  291.4 12.1 %fusion.35 = f32[256,4096]{1,0:T(8,128)} fusion(bf16[4096,896]{1,0:T(8,128)(2,1)} %all-gather.10.cloned.1.call-done, bf16[4096,896]{1,0:T(8,128)(2,1)} %all-gather.8.cloned.1.call-done, f32[256,896]{1,0:T(8,128)} %fusion.30, bf16[256,4096]{1,0:T(8,128)(2,1)S(1)} %copy-done.3, f32[256]{0:T(256)S(1)} %add_rsqrt_fusion), kind=kOutput, calls=%fused_computation.52 | convolution fusion | flops 3762618368 | bytes 21890048 | tf_op jit(solution)/shard_map/dot_general | solution.py:70
  303.5 0.0 all-gather.12.cloned.1.call-update
  303.6 0.0 reduce-scatter.2.cloned.1.call-start
  303.6 0.9 copy-done.13
  304.5 3.8 convolution_convert_fusion.1
  308.4 0.0 copy-start.19
  308.4 1.5 convolution_convert_fusion.2
  309.9 0.8 fusion.38
  310.7 0.1 copy-done.6
  310.8 2.7 collective-permute-start.2
  313.5 4.9 convolution_convert_fusion
  318.4 3.3 reshape.198
  321.8 0.1 add_compare_fusion
  321.9 0.4 fusion.16
  322.3 1.5 and_and_fusion
  323.8 2.2 broadcast_and_fusion
  326.0 4.5 convolution_convert_fusion.3
  330.5 0.0 collective-permute-done.2
  330.5 2.5 pad_maximum_fusion
  333.1 2.7 reshape.191
  335.7 2.6 reshape.192
  338.4 1.6 constant_dynamic-update-slice_fusion.1
  340.0 1.6 constant_dynamic-update-slice_fusion
  341.6 0.7 fusion.51
  342.4 1.3 copy.20
  343.7 1.4 copy.18
  345.0 11.0 %fusion.54 = (f32[4,2,512]{2,1,0:T(2,128)S(1)}, f32[4,2,512,1024]{3,2,1,0:T(8,128)}) fusion(pred[4,512,1024]{2,1,0:T(8,128)(4,1)} %broadcast_and_fusion, bf16[4,1024,2,64]{1,3,2,0:T(8,128)(2,1)} %bitcast.49, bf16[4,512,2,64]{3,2,1,0:T(2,128)(2,1)} %reshape.198), kind=kOutput, calls=%fused_computation.79 | convolution fusion | flops 553649152 | bytes 20463616 | tf_op jit(solution)/shard_map/sub | solution.py:41
  356.0 104.2 %all-gather.12.cloned.1.call-done = f32[2048,4096]{1,0:T(8,128)} async-done(((f32[256,4096]{1,0:T(8,128)}), f32[2048,4096]{1,0:T(8,128)}) %all-gather.12.cloned.1.call-update) | async-done | bytes 33554448 | tf_op jit(solution)/shard_map/all_gather | solution.py:76
  460.2 14.3 %reduce_sum.37 = f32[256,4096]{1,0:T(8,128)} reduce(f32[8,256,4096]{2,1,0:T(8,128)} %bitcast.45, f32[]{:T(128)} %constant.15.clone.1), dimensions={0}, to_apply=%region_1.2 | reduce | flops 7340032 | bytes 37748740 | tf_op jit(solution)/shard_map/reduce_sum | solution.py:76
  474.5 3.1 convolution_convert_fusion.4
  477.7 0.3 copy-done.1
  478.0 0.3 copy-done.8
  478.3 0.9 convolution_convert_fusion.5
  479.2 0.1 fusion.39
  479.2 3.1 collective-permute-start
  482.4 1.3 collective-permute-start.1
  483.7 0.0 copy-start.11
  483.7 8.6 %fusion.21 = bf16[4,512,2,64]{1,3,2,0:T(8,128)(2,1)S(1)} fusion(bf16[4,1024,2,64]{1,3,2,0:T(8,128)(2,1)S(1)} %bitcast.48, f32[4,2,512,1024]{3,2,1,0:T(8,128)} %get-tuple-element.14, f32[4,2,512]{2,1,0:T(2,128)S(1)} %get-tuple-element.13), kind=kOutput, calls=%fused_computation.39 | convolution fusion | flops 545521664 | bytes 18366464 | tf_op jit(solution)/shard_map/bhqk,bkhd->bqhd/dot_general | solution.py:149
  492.3 0.4 copy.22
  492.7 0.1 copy.25
  492.8 0.0 collective-permute-done
  492.9 0.1 pad_maximum_fusion.3
  493.0 0.7 fusion.52
  493.7 1.8 fusion.53
  495.5 0.0 copy-start.16
  495.5 3.5 fusion.15
  499.0 0.0 copy-start.12
  499.1 1.3 fusion.59
  500.3 4.5 convolution_add_fusion
  504.9 0.0 reduce-scatter.2.cloned.1.call-update
  504.9 57.5 %reduce-scatter.2.cloned.1.call-done = f32[2048,128]{1,0:T(8,128)} async-done(((f32[2048,1024]{1,0:T(8,128)}), f32[2048,128]{1,0:T(8,128)}) %reduce-scatter.2.cloned.1.call-update) | async-done | bytes 1048592 | tf_op jit(solution)/shard_map/reduce_scatter | solution.py:156
  562.4 2.1 convert_element_type.68
  (39 shorter events, 0.1 us)
Async XLA Ops:
  6.5 468.0 %copy-start = (bf16[4096,128]{1,0:T(8,128)(2,1)S(1)}, bf16[4096,128]{1,0:T(8,128)(2,1)}, u32[]{:S(2)}) copy-start(bf16[4096,128]{1,0:T(8,128)(2,1)} %param.19) | copy-start | bytes 3145732
  6.5 99.6 %all-gather.6.cloned.1.call-start = ((), (), s32[]{:S(2)}) async-start(), calls=%async_computation.1 | async-start | bytes 7569408 | tf_op jit(solution)/shard_map/all_gather | solution.py:67
  7.3 191.5 %all-gather.10.cloned.1.call-start = ((), (), s32[]{:S(2)}) async-start(), calls=%async_computation.3 | async-start | bytes 7569408 | tf_op jit(solution)/shard_map/all_gather | solution.py:72
  8.0 283.4 %all-gather.8.cloned.1.call-start = ((), (), s32[]{:S(2)}) async-start(), calls=%async_computation.2 | async-start | bytes 7569408 | tf_op jit(solution)/shard_map/all_gather | solution.py:68
  8.7 451.5 %all-gather.12.cloned.1.call-start = ((), (), s32[]{:S(2)}) async-start(), calls=%async_computation.5 | async-start | bytes 37748736 | tf_op jit(solution)/shard_map/all_gather | solution.py:76
  10.9 280.5 %copy-start.3 = (bf16[256,4096]{1,0:T(8,128)(2,1)S(1)}, bf16[256,4096]{1,0:T(8,128)(2,1)}, u32[]{:S(2)}) copy-start(bf16[256,4096]{1,0:T(8,128)(2,1)} %param.14) | copy-start | bytes 6291460
  303.5 0.9 copy-start.13
  303.6 258.8 %reduce-scatter.2.cloned.1.call-start = ((), (), s32[]{:S(2)}) async-start(), calls=%async_computation.4 | async-start | bytes 9437184 | tf_op jit(solution)/shard_map/reduce_scatter | solution.py:156
  304.5 3.9 copy-start.2
  304.5 3.9 copy-start.14
  308.4 1.5 copy-start.4
  308.4 5.1 copy-start.19
  309.9 0.9 copy-start.6
  310.8 11.0 %copy-start.18 = (s32[2048]{0:T(1024)S(1)}, s32[2048]{0:T(1024)}, u32[]{:S(2)}) copy-start(s32[2048]{0:T(1024)} %param.21) | copy-start | bytes 24580
  310.8 19.7 %collective-permute-start.2 = (bf16[512,256]{0,1:T(8,128)(2,1)}, bf16[512,256]{0,1:T(8,128)(2,1)}, u32[]{:S(2)}, u32[]{:S(2)}) collective-permute-start(bf16[512,256]{0,1:T(8,128)(2,1)} %fusion.38), channel_id=1, source_target_pairs={{0,8},{8,16},{16,24},{24,32},{32,40},{40,48},{48,56},{56,64},{64,7... | collective-permute-start | bytes 786440 | tf_op jit(solution)/shard_map/ppermute | solution.py:30
  318.4 7.6 %copy-start.15 = (bf16[1024,128]{1,0:T(8,128)(2,1)S(1)}, bf16[1024,128]{1,0:T(8,128)(2,1)}, u32[]{:S(2)}) copy-start(bf16[1024,128]{1,0:T(8,128)(2,1)} %param.22) | copy-start | bytes 786436
  322.3 8.3 %copy-start.5 = (bf16[2048,128]{0,1:T(8,128)(2,1)S(1)}, bf16[2048,128]{0,1:T(8,128)(2,1)}, u32[]{:S(2)}) copy-start(bf16[2048,128]{0,1:T(8,128)(2,1)} %copy-done.4) | copy-start | bytes 1572868
  322.3 8.3 %copy-start.7 = (bf16[2048,128]{0,1:T(8,128)(2,1)S(1)}, bf16[2048,128]{0,1:T(8,128)(2,1)}, u32[]{:S(2)}) copy-start(bf16[2048,128]{0,1:T(8,128)(2,1)} %copy-done.6) | copy-start | bytes 1572868
  474.5 3.4 copy-start.1
  474.5 3.7 copy-start.8
  478.3 5.4 copy-start.9
  479.2 13.6 %collective-permute-start = (bf16[23,256]{0,1:T(8,128)(2,1)S(1)}, bf16[23,256]{0,1:T(8,128)(2,1)S(1)}, u32[]{:S(2)}, u32[]{:S(2)}) collective-permute-start(bf16[23,256]{0,1:T(8,128)(2,1)S(1)} %get-tuple-element.11), channel_id=1, source_target_pairs={{0,8},{8,16},{16,24},{24,32},{32,40},{40,48},{48,56},{56,64},{64,7... | collective-permute-start | bytes 35336 | tf_op jit(solution)/shard_map/ppermute | solution.py:21
  482.4 10.5 %collective-permute-start.1 = (bf16[23,256]{0,1:T(8,128)(2,1)S(1)}, bf16[23,256]{0,1:T(8,128)(2,1)S(1)}, u32[]{:S(2)}, u32[]{:S(2)}) collective-permute-start(bf16[23,256]{0,1:T(8,128)(2,1)S(1)} %get-tuple-element.12), channel_id=1, source_target_pairs={{8,0},{16,8},{24,16},{32,24},{40,32},{48,40},{56,48},{64,56},{72,6... | collective-permute-start | bytes 35336 | tf_op jit(solution)/shard_map/ppermute | solution.py:22
  483.7 10.0 %copy-start.10 = (pred[2048,302]{0,1:T(8,128)(4,1)S(1)}, pred[2048,302]{0,1:T(8,128)(4,1)}, u32[]{:S(2)}) copy-start(pred[2048,302]{0,1:T(8,128)(4,1)} %and_and_fusion) | copy-start | bytes 1855492
  483.7 10.0 %copy-start.11 = (bf16[2048,128]{0,1:T(8,128)(2,1)S(1)}, bf16[2048,128]{0,1:T(8,128)(2,1)}, u32[]{:S(2)}) copy-start(bf16[2048,128]{0,1:T(8,128)(2,1)} %convolution_convert_fusion.3) | copy-start | bytes 1572868
  493.7 1.9 copy-start.17
  495.5 3.5 copy-start.16
  499.0 1.3 copy-start.12
Sparse Core Ops, SparseCore 0:
  9.9 96.1 all-gather.5
  108.7 90.0 all-gather.9
  201.3 90.0 all-gather.7
  303.7 156.5 all-gather.11
  505.0 57.3 reduce-scatter.1
